TPU v7x, 32 devices: a whole 2x2x4 slice. The times are simulated.
32 devices in a mesh: hi: 4 (over x, core), lo: 8 (over z, y).
Axes of the slice: x: 2, y: 2, z: 4, core: 2. Of those that a mesh axis runs over, the one named last changes fastest.
Arguments:
- current: float32 [131072, 256], P(('hi', 'lo')), may hold values from -130 to 130
- signs: int32 [131072], P(('hi', 'lo')), may hold values from -1 to 1, as said below
- sample_rows: int32 [512], P(('hi', 'lo')), may hold values from 0 to 4095
- sample_owner: int32 [512, 1], P(('hi', 'lo')), may hold values from 0 to 7; in each aligned block of 16 rows (0 to 15, 16 to 31, ...) at most 2 rows name the same one
Outputs:
- sketch: float32 [4, 8, 8, 2, 256], P('hi', 'lo')
- r_factor: float32 [256, 256], replicated
- precond: float32 [131072, 256], P(('hi', 'lo'))
Inputs may be any that keep to these rules, and one draw needn't show every extreme that they name: `signs`: each entry is -1 or 1. `sample_owner`: among the 16 samples of one device no owner is named more than 2 times, and in every draw some device names some owner exactly 2 times.
All inputs are finite; a program needn't handle non-finite values.
Results may differ from a plain program's by a relative error of at most 0.000098.
Values sent between devices are 32-bit elements; how exact they have to be, the bound alone decides.
A program may use at most 64 MiB of HBM per device.

v0:
```python
import math

import jax
import jax.numpy as jnp
from jax import lax
from jax.sharding import PartitionSpec as P

MOST = 2


HIGHEST = lax.Precision.HIGHEST


def sylvester(order_size):
    hadamard_table = jnp.ones((1, 1), jnp.float32)
    base_pair = jnp.array([[1.0, 1.0], [1.0, -1.0]], jnp.float32)
    while hadamard_table.shape[0] < order_size:
        hadamard_table = jnp.kron(hadamard_table, base_pair)
    return hadamard_table


def split_order(order_size):
    leading = 2 ** ((order_size.bit_length() - 1) // 2)
    return (leading, order_size // leading)


def shards(current, signs, sample_rows, sample_owner):
    rows_here = current.shape[0]
    panel_width = current.shape[1]
    high_count = lax.axis_size("hi")
    low_count = lax.axis_size("lo")
    devices = high_count * low_count
    count_here = sample_rows.shape[0]
    scale_all = 1.0 / math.sqrt(rows_here * devices)
    signed = current * signs.astype(jnp.float32)[:, None]
    leading, second = split_order(rows_here)
    shaped = signed.reshape(leading, second, panel_width)
    shaped = jnp.einsum("ab,bcp->acp", sylvester(leading), shaped, precision=HIGHEST)
    shaped = jnp.einsum("cd,adp->acp", sylvester(second), shaped, precision=HIGHEST)
    mixture = shaped.reshape(rows_here, panel_width)
    all_samples = lax.all_gather(sample_rows, ("hi", "lo"), axis=0, tiled=True)
    own_device = lax.axis_index("hi") * low_count + lax.axis_index("lo")
    column_signs = lax.dynamic_index_in_dim(sylvester(devices), own_device, 1, keepdims=False)
    row_signs = jnp.repeat(column_signs, count_here)
    shares = jnp.take(mixture, all_samples, axis=0) * row_signs[:, None]
    picked = lax.psum_scatter(shares, ("hi", "lo"), scatter_dimension=0, tiled=True) * scale_all
    owner_ids = sample_owner[:, 0]
    owner_hot = (owner_ids[:, None] == jnp.arange(low_count, dtype=jnp.int32)[None, :]).astype(
        jnp.int32
    )
    before = jnp.cumsum(owner_hot, axis=0) - owner_hot
    slot_ids = jnp.sum(before * owner_hot, axis=1)
    placement = (owner_hot.T[:, None, :] == 1) & (
        slot_ids[None, None, :] == jnp.arange(MOST, dtype=jnp.int32)[None, :, None]
    )
    outgoing = jnp.einsum("omk,kp->omp", placement.astype(jnp.float32), picked, precision=HIGHEST)
    received = lax.all_to_all(outgoing, "lo", split_axis=0, concat_axis=0, tiled=True)
    sketch = received.reshape(1, 1, low_count, MOST, panel_width)
    owned_rows = received.reshape(low_count * MOST, panel_width)
    local_gram = jnp.dot(owned_rows.T, owned_rows, precision=HIGHEST)
    gram_total = lax.psum(local_gram, ("hi", "lo")) * (1.0 / (count_here * devices))
    lower_factor = jnp.linalg.cholesky(gram_total)
    precond = lax.linalg.triangular_solve(
        lower_factor, current, left_side=False, lower=True, transpose_a=True
    )
    return (sketch, lower_factor.T, precond)


def solution(mesh):
    placed = (P(("hi", "lo"), None), P(("hi", "lo")), P(("hi", "lo")), P(("hi", "lo"), None))
    return jax.shard_map(
        shards,
        mesh=mesh,
        in_specs=placed,
        out_specs=(P("hi", "lo", None, None, None), P(), P(("hi", "lo"), None)),
        check_vma=False,
    )
```

profile of v0, /device:TPU:0, one launch (start us, length us, event | category | flops | bytes accessed | tf_op | source)
XLA Modules:
  0.0 434.3 jit_solution(16142233087019374915)
XLA Ops:
  7.2 0.9 dynamic-update-slice.11
  8.1 42.0 %all-reduce.1 = s32[512]{0:T(512)S(1)} all-reduce(s32[512]{0:T(512)S(1)} %dynamic-update-slice.11), channel_id=1, replica_groups=mesh['hi'=4,'lo'=8] {'hi','lo'}, use_global_device_ids=true, to_apply=%add.1 | all-reduce | flops 512 | bytes 4096
  50.1 0.8 broadcast_multiply_fusion.6
  50.9 0.1 mul.371
  51.0 0.8 broadcast_multiply_fusion.5
  51.8 0.1 mul.375
  51.8 0.7 convert_element_type.16
  52.6 0.8 broadcast_multiply_fusion.4
  53.3 0.1 mul.379
  53.4 0.8 broadcast_multiply_fusion.3
  54.2 0.1 mul.383
  54.3 0.9 broadcast_multiply_fusion.1
  55.2 0.2 dynamic-slice_reduce_fusion
  55.5 0.1 mul.427
  55.6 0.7 reshape.344
  56.2 2.6 broadcast_multiply_fusion
  58.8 6.3 %fusion.2 = f32[64,64,256]{2,0,1:T(8,128)S(1)} fusion(f32[64,64,1]{1,0,2:T(8,128)S(1)} %reshape.344, f32[64,64,256]{2,1,0:T(8,128)S(1)} %bitcast.55), kind=kOutput, calls=%fused_computation.7 | convolution fusion | flops 805306368 | bytes 8404992 | tf_op jit(solution)/shard_map/ab,bcp->acp/dot_general | solution.py:38
  65.1 7.0 %fusion = f32[64,256,64]{1,2,0:T(8,128)} fusion(f32[64,64,1]{1,0,2:T(8,128)S(1)} %reshape.344, f32[64,64,256]{2,0,1:T(8,128)S(1)} %fusion.2), kind=kOutput, calls=%fused_computation.5 | convolution fusion | flops 805306368 | bytes 8404992 | tf_op jit(solution)/shard_map/cd,adp->acp/dot_general | solution.py:39
  72.2 3.8 gather_fusion
  75.9 1.0 select_multiply_fusion
  77.1 0.2 select_reduce_fusion.2
  77.3 135.4 %reduce-scatter.2.cloned.1.call-done = f32[16,256]{1,0:T(8,128)} async-done(((f32[512,256]{1,0:T(8,128)}), f32[16,256]{1,0:T(8,128)}) %reduce-scatter.2.cloned.1.call-update) | async-done | bytes 16400 | tf_op jit(solution)/shard_map/reduce_scatter | solution.py:46
  212.7 0.8 fusion.14
  213.6 8.9 %all_to_all.5 = f32[8,2,256]{2,1,0:T(2,128)S(1)} all-to-all(f32[8,2,256]{2,1,0:T(2,128)S(1)} %copy.33), channel_id=1, replica_groups=mesh['hi'=4,'lo'=8] {'lo'}, dimensions={0} | all-to-all | bytes 32768 | tf_op jit(solution)/shard_map/all_to_all | solution.py:57
  222.5 1.1 convolution_bitcast_fusion
  223.7 123.2 %all-reduce.4.cloned.1.call-done = f32[256,256]{0,1:T(8,128)} async-done(((f32[256,256]{0,1:T(8,128)}), f32[256,256]{0,1:T(8,128)}) %all-reduce.4.cloned.1.call-update) | async-done | bytes 262160 | tf_op jit(solution)/shard_map/psum | solution.py:61
  346.9 1.0 broadcast_multiply_fusion.2
  347.8 0.1 copy.37
  348.0 1.0 fusion.6
  349.0 11.7 %cholesky.50 = f32[128,128]{1,0:T(8,128)S(1)} custom-call(f32[128,128]{1,0:T(8,128)S(1)} %cholesky.118), custom_call_target="Cholesky" | custom-call | tf_op jit(solution)/shard_map/jit(cholesky)/cholesky | solution.py:62
  360.7 9.8 %custom-call.14 = f32[1,128,128]{1,2,0:T(8,128)S(1)} custom-call(f32[1,128,128]{2,1,0:T(8,128)S(1)} %get-tuple-element.38), custom_call_target="InvertDiagBlocksLowerTriangular" | custom-call | tf_op jit(solution)/shard_map/jit(cholesky)/cholesky | solution.py:62
  370.6 0.2 constant_dynamic-update-slice_fusion.1
  370.8 0.3 convolution_subtract_fusion.1
  371.0 11.7 %cholesky.105 = f32[128,128]{1,0:T(8,128)S(1)} custom-call(f32[128,128]{1,0:T(8,128)S(1)} %convolution_subtract_fusion.1), custom_call_target="Cholesky" | custom-call | tf_op jit(solution)/shard_map/jit(cholesky)/cholesky | solution.py:62
  382.8 0.6 compare_reduce_fusion
  384.8 0.8 copy.38
  385.7 4.1 while.1
  385.7 0.6 fusion.32
  386.3 1.4 bitcast_dynamic-update-slice_fusion.2
  387.7 0.6 fusion.32
  388.3 1.4 bitcast_dynamic-update-slice_fusion.2
  389.8 19.9 %custom-call.15 = f32[2,128,128]{1,2,0:T(8,128)S(1)} custom-call(f32[2,128,128]{2,1,0:T(8,128)S(1)} %get-tuple-element.10), custom_call_target="InvertDiagBlocksLowerTriangular" | custom-call | tf_op jit(solution)/shard_map/triangular_solve | solution.py:63
  409.7 3.7 fusion.4
  413.4 3.4 convolution_subtract_fusion
  416.8 2.0 fusion.9
  418.9 2.4 pad_maximum_fusion
  421.3 5.6 %copy.39 = f32[4096,256]{1,0:T(8,128)} copy(f32[4096,256]{0,1:T(8,128)} %pad_maximum_fusion) | data formatting | bytes 8388608
  426.8 0.6 copy.62
  (28 shorter events, 0.6 us)
Async XLA Ops:
  7.2 205.6 %reduce-scatter.2.cloned.1.call-start = ((), (), s32[]{:S(2)}) async-start(), calls=%async_computation.2 | async-start | bytes 540672 | tf_op jit(solution)/shard_map/reduce_scatter | solution.py:46
  72.2 4.9 %copy-start.1 = (s32[16,1]{0,1:T(1,128)S(1)}, s32[16,1]{0,1:T(1,128)}, u32[]{:S(2)}) copy-start(s32[16,1]{0,1:T(1,128)} %param.10) | copy-start | bytes 196
  77.0 269.9 %all-reduce.4.cloned.1.call-start = ((), (), s32[]{:S(2)}) async-start(), calls=%async_computation.3 | async-start | bytes 524288 | tf_op jit(solution)/shard_map/psum | solution.py:61
  409.7 3.7 copy-start
Sparse Core Ops, SparseCore 0:
  77.1 135.6 reduce-scatter.1
  223.8 123.0 all-reduce.3
where the time goes:
time: 435 us; the launch traced here: 434 us
  waiting for transfers between devices  259 us (60%)
  other arithmetic  66.9 us (15%)
  blocking collectives  50.9 us (12%)
  matrix products  24.9 us (6%)
  local copies, waits for them, and re-layouts  17.4 us (4%)
  between operations  15.6 us (4%)
    reduce_scatter x1, waiting for transfers between devices, shards(): lax.psum_scatter(shares, ('hi', 'lo'), scatter_dimension=0, tiled=True)  135 us
    psum x1, waiting for transfers between devices, shards(): lax.psum(local_gram, ('hi', 'lo')) * (1.0 / (count_here * devices))  123 us
    unnamed x1, blocking collectives  42 us
    another operation x6, other arithmetic, shards(): lower_factor = jnp.linalg.cholesky(gram_total)  34 us
    another operation x4, other arithmetic, shards(): lax.linalg.triangular_solve(lower_factor, current, left_side=False, lower...  22.3 us
    another operation x3, matrix products, shards(): lax.linalg.triangular_solve(lower_factor, current, left_side=False, lower...  9.13 us
    all_to_all x1, blocking collectives, shards(): lax.all_to_all(outgoing, 'lo', split_axis=0, concat_axis=0, tiled=True)  8.94 us
  transfers between devices with their start and end apart: 2, of which 2 were waited for; matrix products, arithmetic and copies ran while one was open for 0% of the time, Pallas kernels for 0%

commit v1 on v0

v1 whole, which is shorter than its diff:
```python
import functools
import math

import jax
import jax.numpy as jnp
from jax import lax
from jax.experimental import pallas as pl
from jax.experimental.pallas import tpu as pltpu
from jax.sharding import PartitionSpec as P

MOST = 2
LANES = 128
BLOCK = 64
MESH = pl.DeviceIdType.MESH
HIGHEST = lax.Precision.HIGHEST
F32 = jnp.float32
BF16 = jnp.bfloat16


def bits_of(size):
    return size.bit_length() - 1


def reverse_bits(value, width):
    out = 0
    for bit in range(width):
        out |= ((value >> bit) & 1) << (width - 1 - bit)
    return out


def parity(value, top):
    shift = 1
    while shift * 2 < top:
        shift *= 2
    while shift >= 1:
        value = value ^ (value >> shift)
        shift //= 2
    return value & 1


def mix_kernel(nh, nl, count, note_ref, signs_ref, current_ref, gram_ref, sketch_ref,
               xbuf, xhi, xlo, notes, mat, share, landed, gathered,
               load_sem, nsend, nrecv, rsend, rrecv, gsend, grecv):
    hi, lo = lax.axis_index("hi"), lax.axis_index("lo")
    own = hi * nl + lo
    bh, bl = bits_of(nh), bits_of(nl)
    stages = bh + bl
    devices = nh * nl
    rows, width = current_ref.shape
    total = devices * count
    row_bits = bits_of(rows)
    loads = 8
    step = rows // loads

    def load(c):
        at = pl.ds(c * step, step)
        return pltpu.make_async_copy(current_ref.at[at, :], xbuf.at[at, :], load_sem.at[c])

    for c in range(loads):
        load(c).start()

    def peer(t):
        return (hi ^ (t >> bl), lo ^ (t & (nl - 1)))

    def place(t):
        return (reverse_bits(t >> bl, bh) << bl) | reverse_bits(t & (nl - 1), bl)

    barrier = pltpu.get_barrier_semaphore()
    for t in range(1, devices):
        pl.semaphore_signal(barrier, inc=1, device_id=peer(t), device_id_type=MESH)
    pl.semaphore_wait(barrier, devices - 1)

    def note(t):
        return pltpu.make_async_remote_copy(
            src_ref=note_ref, dst_ref=notes.at[pl.ds(place(t), 1), :],
            send_sem=nsend.at[t], recv_sem=nrecv.at[t],
            device_id=peer(t), device_id_type=MESH)

    for t in range(1, devices):
        note(t).start()
    notes[0:1, :] = note_ref[...]
    for c in range(loads):
        load(c).wait()

        @pl.loop(0, step // 64)
        def _(r):
            at = pl.ds(pl.multiple_of(c * step + r * 64, 64), 64)
            x = xbuf[at, :]
            top = x.astype(BF16)
            xhi[at, :] = top
            xlo[at, :] = (x - top.astype(F32)).astype(BF16)

    for t in range(1, devices):
        note(t).wait()

    chunk = min(256, total // 2)
    groups = chunk // count
    lane = lax.broadcasted_iota(jnp.int32, (chunk, LANES), 1)
    line = lax.broadcasted_iota(jnp.int32, (chunk, LANES), 0)

    def mix(first):
        part = notes[pl.ds(pl.multiple_of(first // count, groups), groups), :]
        wide = jnp.broadcast_to(part[:, None, :], (groups, count, LANES)).reshape(chunk, LANES)
        wide = jnp.where(lane == line % count, wide, 0.0)
        index = jnp.broadcast_to(jnp.sum(wide, axis=1, keepdims=True), (chunk, LANES))
        index = index.astype(jnp.int32)
        base = parity(index & (own * rows + lane), 2 ** (row_bits + stages).bit_length())
        base = (1 - 2 * base).astype(F32).astype(BF16)
        factors = []
        for bit in range(bits_of(rows // LANES)):
            flag = (index >> (bits_of(LANES) + bit)) & 1
            factors.append((1 - 2 * flag).astype(F32).astype(BF16))
        made = {0: base}
        for b in range(rows // LANES):
            if b:
                low = b & -b
                made[b] = made[b - low] * factors[bits_of(low)]
            sign = signs_ref[b:b + 1, :].astype(F32).astype(BF16)
            mat[:, b * LANES:(b + 1) * LANES] = made[b] * sign
        out = jnp.dot(mat[...], xhi[...], preferred_element_type=F32)
        out = out + jnp.dot(mat[...], xlo[...], preferred_element_type=F32)
        share[pl.ds(pl.multiple_of(first, chunk), chunk), :] = out

    def mix_range(first, last):
        if last - first == chunk:
            mix(first)
        else:
            @pl.loop(0, (last - first) // chunk)
            def _(k):
                mix(first + k * chunk)

    def stage_peer(s):
        return peer(1 << (bl + s)) if s < bh else peer(1 << (s - bh))

    def halve(s):
        half = total >> (s + 1)
        return pltpu.make_async_remote_copy(
            src_ref=share.at[pl.ds(half, half), :],
            dst_ref=landed.at[pl.ds(half, half), :],
            send_sem=rsend.at[s], recv_sem=rrecv.at[s],
            device_id=stage_peer(s), device_id_type=MESH)

    half = total // 2
    mix_range(half, total)
    halve(0).start()
    mix_range(0, half)
    for s in range(stages):
        half = total >> (s + 1)
        halve(s).wait_recv()
        if s < stages - 1:
            quarter = half // 2
            share[quarter:half, :] = share[quarter:half, :] + landed[half + quarter:half + half, :]
            halve(s + 1).start()
            share[0:quarter, :] = share[0:quarter, :] + landed[half:half + quarter, :]
        else:
            scale_all = 1.0 / math.sqrt(rows * devices)
            gathered[0:half, :] = (share[0:half, :] + landed[half:half + half, :]) * scale_all

    def double(s):
        size = total >> (s + 1)
        return pltpu.make_async_remote_copy(
            src_ref=gathered.at[pl.ds(0, size), :],
            dst_ref=gathered.at[pl.ds(size, size), :],
            send_sem=gsend.at[s], recv_sem=grecv.at[s],
            device_id=stage_peer(s), device_id_type=MESH)

    def product(first, size):
        block = gathered[first:first + size, :]
        return lax.dot_general(block, block, (((0,), (0,)), ((), ())),
                               precision=HIGHEST, preferred_element_type=F32)

    def sketch():
        span = nl * count
        owners = notes[0:nl, :]
        q = lax.broadcasted_iota(jnp.int32, (nl, LANES), 0)
        k = lax.broadcasted_iota(jnp.int32, (nl, LANES), 1)
        mine = (owners == lo.astype(F32)) & (k >= count) & (k < 2 * count)
        match = jnp.where(mine, 1.0, 0.0).astype(F32)
        up = lax.broadcasted_iota(jnp.int32, (LANES, LANES), 0)
        across = lax.broadcasted_iota(jnp.int32, (LANES, LANES), 1)
        ahead = jnp.where(up < across, 1.0, 0.0).astype(F32)
        before = jnp.dot(match, ahead, precision=HIGHEST, preferred_element_type=F32)
        spread_row = lax.broadcasted_iota(jnp.int32, (LANES, span), 0)
        spread_col = lax.broadcasted_iota(jnp.int32, (LANES, span), 1)
        spread = jnp.where(spread_row - count == spread_col % count, 1.0, 0.0).astype(F32)
        lead = lax.broadcasted_iota(jnp.int32, (nl, span), 0)
        cell = lax.broadcasted_iota(jnp.int32, (nl, span), 1)
        order_row = lax.broadcasted_iota(jnp.int32, (nl, nl), 0)
        order_col = lax.broadcasted_iota(jnp.int32, (nl, nl), 1)
        source = jnp.zeros((nl, nl), jnp.int32)
        for bit in range(bl):
            source = source | (((order_col >> bit) & 1) << (bl - 1 - bit))
        turn = jnp.where((source ^ lo) == order_row, 1.0, 0.0).astype(F32)
        rows_here = gathered[0:span, :]
        for m in range(MOST):
            chosen = jnp.where(jnp.abs(before - m) < 0.5, match, 0.0)
            wide = jnp.dot(chosen, spread, precision=HIGHEST, preferred_element_type=F32)
            wide = jnp.where(cell // count == lead, wide, 0.0)
            wide = jnp.dot(turn, wide, precision=HIGHEST, preferred_element_type=F32)
            sketch_ref[m, :, :] = jnp.dot(wide, rows_here, precision=HIGHEST,
                                          preferred_element_type=F32)

    for s in reversed(range(stages)):
        size = total >> (s + 1)
        double(s).start()
        if s == stages - 1:
            for r in range(stages):
                halve(r).wait_send()
        if s == bh - 1:
            sketch()
        if s == 0:
            gram_ref[...] = product(0, size)
        double(s).wait()
        if s == 0:
            gram_ref[...] = (gram_ref[...] + product(size, size)) * (1.0 / total)


def factor_kernel(gram_ref, sketch_in, current_ref, sketch_ref, r_ref, out_ref,
                  xbuf, obuf, load_sem, store_sem):
    rows, width = current_ref.shape
    pieces = 8
    step = rows // pieces

    def load(c):
        at = pl.ds(c * step, step)
        return pltpu.make_async_copy(current_ref.at[at, :], xbuf.at[at, :], load_sem.at[c])

    def store(c):
        at = pl.ds(c * step, step)
        return pltpu.make_async_copy(obuf.at[at, :], out_ref.at[at, :], store_sem.at[c])

    for c in range(pieces):
        load(c).start()
    for source in range(sketch_ref.shape[0]):
        for m in range(MOST):
            sketch_ref[source, m:m + 1, :] = sketch_in[m, source:source + 1, :]

    n = width
    blocks = n // BLOCK
    row = lax.broadcasted_iota(jnp.int32, (BLOCK, n), 0)
    col = lax.broadcasted_iota(jnp.int32, (BLOCK, n), 1)
    a = [gram_ref[k * BLOCK:(k + 1) * BLOCK, :] for k in range(blocks)]
    w = [jnp.where(row + k * BLOCK == col, 1.0, 0.0).astype(F32) for k in range(blocks)]
    sub = lax.broadcasted_iota(jnp.int32, (8, 2 * BLOCK), 0)
    small_row = lax.broadcasted_iota(jnp.int32, (BLOCK, BLOCK), 0)
    small_col = lax.broadcasted_iota(jnp.int32, (BLOCK, BLOCK), 1)
    unit = jnp.where(small_row == small_col, 1.0, 0.0).astype(F32)
    for k in range(blocks):
        at = slice(k * BLOCK, (k + 1) * BLOCK)
        both = jnp.concatenate([a[k][:, at], unit], axis=1)
        tiles = [both[8 * g:8 * g + 8, :] for g in range(BLOCK // 8)]
        for i in range(BLOCK - 1):
            g0, r0 = i // 8, i % 8
            pivot = tiles[g0][r0:r0 + 1, :]
            scaled = pivot / tiles[g0][r0:r0 + 1, i:i + 1]
            for g in range(g0, BLOCK // 8):
                if g == g0 and r0 == 7:
                    continue
                drop = tiles[g][:, i:i + 1] * scaled
                if g == g0:
                    drop = jnp.where(sub > r0, drop, 0.0)
                tiles[g] = tiles[g] - drop
        both = jnp.concatenate(tiles, axis=0)
        diag = jnp.sum(jnp.where(small_row == small_col, both[:, :BLOCK], 0.0), axis=1, keepdims=True)
        scale = 1.0 / jnp.sqrt(diag)
        inv = both[:, BLOCK:] * scale
        r_rows = jnp.dot(inv, a[k], precision=HIGHEST, preferred_element_type=F32)
        w_rows = jnp.dot(inv, w[k], precision=HIGHEST, preferred_element_type=F32)
        for later in range(k + 1, blocks):
            lower = lax.dot_general(a[later][:, at], inv, (((1,), (1,)), ((), ())),
                                    precision=HIGHEST, preferred_element_type=F32)
            a[later] = a[later] - jnp.dot(lower, r_rows, precision=HIGHEST, preferred_element_type=F32)
            w[later] = w[later] - jnp.dot(lower, w_rows, precision=HIGHEST, preferred_element_type=F32)
        r_ref[at, :] = jnp.where(row + k * BLOCK <= col, r_rows, 0.0)
        w[k] = w_rows
    inverse = jnp.concatenate(w, axis=0).T
    top = inverse.astype(BF16)
    rest = (inverse - top.astype(F32)).astype(BF16)
    for c in range(pieces):
        load(c).wait()
        at = slice(c * step, (c + 1) * step)
        x = xbuf[at, :]
        x_top = x.astype(BF16)
        x_rest = (x - x_top.astype(F32)).astype(BF16)
        y = jnp.dot(x_top, rest, preferred_element_type=F32)
        y = y + jnp.dot(x_rest, top, preferred_element_type=F32)
        y = y + jnp.dot(x_top, top, preferred_element_type=F32)
        obuf[at, :] = y
        store(c).start()
    for c in range(pieces):
        store(c).wait()


def shards(nh, nl, current, signs, sample_rows, sample_owner):
    rows, width = current.shape
    count = sample_rows.shape[0]
    devices = nh * nl
    total = devices * count
    stages = bits_of(devices)
    own = lax.axis_index("hi") * nl + lax.axis_index("lo")
    note = jnp.concatenate([own * rows + sample_rows, sample_owner[:, 0]])
    note = jnp.pad(note.astype(F32), (0, LANES - 2 * count))[None, :]
    vmem = pl.BlockSpec(memory_space=pltpu.VMEM)
    anywhere = pl.BlockSpec(memory_space=pl.ANY)
    dma = pltpu.SemaphoreType.DMA
    chunk = min(256, total // 2)
    gram, picked = pl.pallas_call(
        functools.partial(mix_kernel, nh, nl, count),
        name="mix",
        out_shape=(jax.ShapeDtypeStruct((width, width), F32),
                   jax.ShapeDtypeStruct((MOST, nl, width), F32)),
        in_specs=[vmem, vmem, anywhere],
        out_specs=(vmem, vmem),
        scratch_shapes=[
            pltpu.VMEM((rows, width), F32),
            pltpu.VMEM((rows, width), BF16),
            pltpu.VMEM((rows, width), BF16),
            pltpu.VMEM((devices, LANES), F32),
            pltpu.VMEM((chunk, rows), BF16),
            pltpu.VMEM((total, width), F32),
            pltpu.VMEM((total, width), F32),
            pltpu.VMEM((total, width), F32),
            dma((8,)), dma((devices,)), dma((devices,)),
            dma((stages,)), dma((stages,)), dma((stages,)), dma((stages,)),
        ],
        compiler_params=pltpu.CompilerParams(
            collective_id=0, has_side_effects=True, vmem_limit_bytes=48 * 2 ** 20),
    )(note, signs.reshape(rows // LANES, LANES), current)
    sketch, r_factor, precond = pl.pallas_call(
        factor_kernel,
        name="factor",
        out_shape=(jax.ShapeDtypeStruct((nl, MOST, width), F32),
                   jax.ShapeDtypeStruct((width, width), F32),
                   jax.ShapeDtypeStruct((rows, width), F32)),
        in_specs=[vmem, vmem, anywhere],
        out_specs=(vmem, vmem, anywhere),
        scratch_shapes=[
            pltpu.VMEM((rows, width), F32),
            pltpu.VMEM((rows, width), F32),
            dma((8,)), dma((8,)),
        ],
        compiler_params=pltpu.CompilerParams(vmem_limit_bytes=48 * 2 ** 20),
    )(gram, picked, current)
    return (sketch.reshape(1, 1, nl, MOST, width), r_factor, precond)


def solution(mesh):
    placed = (P(("hi", "lo"), None), P(("hi", "lo")), P(("hi", "lo")), P(("hi", "lo"), None))
    return jax.shard_map(
        functools.partial(shards, mesh.shape["hi"], mesh.shape["lo"]),
        mesh=mesh,
        in_specs=placed,
        out_specs=(P("hi", "lo", None, None, None), P(), P(("hi", "lo"), None)),
        check_vma=False,
    )
```

time: 435 us -> 80.7 us (0.19)
  waiting for transfers between devices: 259 us -> 0 us
  Pallas kernels: 0 us -> 75.4 us
  other arithmetic: 66.9 us -> 1.39 us
  blocking collectives: 50.9 us -> 0 us
  matrix products: 24.9 us -> 0 us
  between operations: 15.6 us -> 0.82 us
  local copies, waits for them, and re-layouts: 17.4 us -> 2.91 us
    reduce_scatter x1 -> x0, waiting for transfers between devices: 135 us -> none  [shards(): lax.psum_scatter(shares, ('hi', 'lo'), scatter_dimension=0, tiled=True)]
    psum x1 -> x0, waiting for transfers between devices: 123 us -> none  [shards(): lax.psum(local_gram, ('hi', 'lo')) * (1.0 / (count_here * devices))]
    pallas_call x0 -> x2, Pallas kernels: none -> 75.4 us  [the longest x1 44.9 us: shards(): pl.pallas_call(functools.partial(mix_kernel, nh, nl, count), name='mix',...]
    another operation x11 -> x0, other arithmetic: 56.3 us -> none  [the longest x6 34 us: shards(): lower_factor = jnp.linalg.cholesky(gram_total)]
    unnamed x1 -> x0, blocking collectives: 42 us -> none
    dot_general x4 -> x0, matrix products: 15.3 us -> none  [the longest x1 7.05 us: shards(): jnp.einsum('cd,adp->acp', sylvester(second), shaped, precision=HIGHEST)]
    another operation x5 -> x0, matrix products: 9.6 us -> none  [the longest x3 9.13 us: shards(): lax.linalg.triangular_solve(lower_factor, current, left_side=False, lower...]
    all_to_all x1 -> x0, blocking collectives: 8.94 us -> none  [shards(): lax.all_to_all(outgoing, 'lo', split_axis=0, concat_axis=0, tiled=True)]
  transfers between devices with their start and end apart: 2 -> 0, of which waited for: 2 -> 0; matrix products, arithmetic and copies ran while one was open for 0% -> 0% of each run, Pallas kernels for 0% -> 0%
where the time goes in v1:
time: 80.7 us; the launch traced here: 80.5 us
  Pallas kernels  75.4 us (93%)
  local copies, waits for them, and re-layouts  2.91 us (4%)
  other arithmetic  1.39 us (2%)
  between operations  0.82 us (1%)
    pallas_call x1, Pallas kernels, shards(): pl.pallas_call(functools.partial(mix_kernel, nh, nl, count), name='mix',...  44.9 us
    pallas_call x1, Pallas kernels, shards(): pl.pallas_call(factor_kernel, name='factor', out_shape=(jax.ShapeDtypeStr...  30.5 us
    unnamed x6, local copies, waits for them, and re-layouts  2.91 us

profile of v1, /device:TPU:0, one launch (start us, length us, event | category | flops | bytes accessed | tf_op | source)
XLA Modules:
  0.0 80.5 jit_solution(2228366067148881078)
XLA Ops:
  0.6 0.7 broadcast_add_fusion
  1.3 0.7 add_convert_fusion
  2.0 0.0 copy-start
  2.0 2.2 %copy-done = f32[4096,256]{1,0:T(8,128)S(1)} copy-done((f32[4096,256]{1,0:T(8,128)S(1)}, f32[4096,256]{1,0:T(8,128)}, u32[]{:S(2)}) %copy-start) | copy-done | bytes 4194328
  4.2 0.0 copy-start.2
  4.2 0.7 copy-done.2
  4.9 0.0 copy-start.1
  4.9 44.9 %mix.1 = (f32[256,256]{1,0:T(8,128)S(1)}, f32[2,8,256]{2,1,0:T(8,128)S(1)}) custom-call(f32[1,128]{1,0:T(1,128)S(1)} %pad_bitcast_fusion.note_ref, s32[32,128]{1,0:T(8,128)S(1)} %bitcast.5, f32[4096,256]{1,0:T(8,128)S(1)} %copy-done), custom_call_target="tpu_custom_call" | custom-call | tf_op jit(solution)/shard_map/mix/pallas_call | solution.py:307
  49.8 0.0 copy-done.1
  49.8 30.5 %factor.1 = (f32[8,2,256]{2,1,0:T(2,128)}, f32[256,256]{1,0:T(8,128)}, f32[4096,256]{1,0:T(8,128)}) custom-call(f32[256,256]{1,0:T(8,128)S(1)} %get-tuple-element.8.gram_ref, f32[2,8,256]{2,1,0:T(8,128)S(1)} %get-tuple-element.9.sketch_in, f32[4096,256]{1,0:T(8,128)S(1)} %copy-done.1), custom_call_target="tpu_custom_call" | custom-call | tf_op jit(solution)/shard_map/factor/pallas_call | solution.py:329
  (1 shorter events, 0.0 us)
Async XLA Ops:
  2.0 2.2 %copy-start = (f32[4096,256]{1,0:T(8,128)S(1)}, f32[4096,256]{1,0:T(8,128)}, u32[]{:S(2)}) copy-start(f32[4096,256]{1,0:T(8,128)} %current_ref.3) | copy-start | bytes 12582916
  4.2 0.7 copy-start.2
  4.9 44.9 %copy-start.1 = (f32[4096,256]{1,0:T(8,128)S(1)}, f32[4096,256]{1,0:T(8,128)}, u32[]{:S(2)}) copy-start(f32[4096,256]{1,0:T(8,128)} %current_ref.3) | copy-start | bytes 12582916

commit v2 on v1

--- a/solution.py
+++ b/solution.py
@@ -11,6 +11,7 @@
 MOST = 2
 LANES = 128
 BLOCK = 64
+VMEM_LIMIT = 61 * 2 ** 20
 MESH = pl.DeviceIdType.MESH
 HIGHEST = lax.Precision.HIGHEST
 F32 = jnp.float32
@@ -38,9 +39,9 @@
     return value & 1
 
 
-def mix_kernel(nh, nl, count, note_ref, signs_ref, current_ref, gram_ref, sketch_ref,
-               xbuf, xhi, xlo, notes, mat, share, landed, gathered,
-               load_sem, nsend, nrecv, rsend, rrecv, gsend, grecv):
+def mix_kernel(nh, nl, count, rows_ref, owner_ref, signs_ref, current_ref, gram_ref, sketch_ref,
+               note_ref, xbuf, xhi, xlo, notes, mat, share, landed, shared, gathered,
+               load_sem, nsend, nrecv, rsend, rrecv, lsend, lrecv, asend, arecv, gsend, grecv):
     hi, lo = lax.axis_index("hi"), lax.axis_index("lo")
     own = hi * nl + lo
     bh, bl = bits_of(nh), bits_of(nl)
@@ -58,6 +59,13 @@
 
     for c in range(loads):
         load(c).start()
+
+    tags = lax.broadcasted_iota(jnp.int32, (count, LANES), 1)
+    spots = lax.broadcasted_iota(jnp.int32, (count, LANES), 0)
+    named = jnp.broadcast_to(owner_ref[...].astype(F32), (count, LANES))
+    named = jnp.where(tags == spots + count, named, 0.0)
+    note_ref[...] = jnp.sum(named, axis=0, keepdims=True)
+    note_ref[:, 0:count] = (rows_ref[...] + own * rows).astype(F32)
 
     def peer(t):
         return (hi ^ (t >> bl), lo ^ (t & (nl - 1)))
@@ -140,29 +148,57 @@
             send_sem=rsend.at[s], recv_sem=rrecv.at[s],
             device_id=stage_peer(s), device_id_type=MESH)
 
+    span = nl * count
     half = total // 2
     mix_range(half, total)
     halve(0).start()
     mix_range(0, half)
-    for s in range(stages):
+    for s in range(bh):
         half = total >> (s + 1)
+        quarter = half // 2
         halve(s).wait_recv()
-        if s < stages - 1:
-            quarter = half // 2
-            share[quarter:half, :] = share[quarter:half, :] + landed[half + quarter:half + half, :]
+        share[quarter:half, :] = share[quarter:half, :] + landed[half + quarter:half + half, :]
+        if s < bh - 1:
             halve(s + 1).start()
-            share[0:quarter, :] = share[0:quarter, :] + landed[half:half + quarter, :]
-        else:
-            scale_all = 1.0 / math.sqrt(rows * devices)
-            gathered[0:half, :] = (share[0:half, :] + landed[half:half + half, :]) * scale_all
-
-    def double(s):
-        size = total >> (s + 1)
+        share[0:quarter, :] = share[0:quarter, :] + landed[half:half + quarter, :]
+
+    def low_sum(t):
         return pltpu.make_async_remote_copy(
-            src_ref=gathered.at[pl.ds(0, size), :],
-            dst_ref=gathered.at[pl.ds(size, size), :],
-            send_sem=gsend.at[s], recv_sem=grecv.at[s],
+            src_ref=share.at[pl.ds(place(t) * count, count), :],
+            dst_ref=shared.at[t],
+            send_sem=lsend.at[t], recv_sem=lrecv.at[t],
+            device_id=peer(t), device_id_type=MESH)
+
+    def low_gather(t):
+        return pltpu.make_async_remote_copy(
+            src_ref=gathered.at[pl.ds(0, count), :],
+            dst_ref=gathered.at[pl.ds(place(t) * count, count), :],
+            send_sem=asend.at[t], recv_sem=arecv.at[t],
+            device_id=peer(t), device_id_type=MESH)
+
+    for t in reversed(range(1, nl)):
+        low_sum(t).start()
+    kept = share[0:count, :]
+    for t in range(1, nl):
+        low_sum(t).wait_recv()
+        kept = kept + shared[t]
+    gathered[0:count, :] = kept * (1.0 / math.sqrt(rows * devices))
+    for t in reversed(range(1, nl)):
+        low_gather(t).start()
+    for t in range(1, nl):
+        low_sum(t).wait_send()
+    for r in range(bh):
+        halve(r).wait_send()
+
+    def pass_on(q, s):
+        return pltpu.make_async_remote_copy(
+            src_ref=gathered.at[pl.ds(q * span, span), :],
+            dst_ref=gathered.at[pl.ds((q + (nh >> (s + 1))) * span, span), :],
+            send_sem=gsend.at[s * nh + q], recv_sem=grecv.at[s * nh + q],
             device_id=stage_peer(s), device_id_type=MESH)
+
+    def came_by(q):
+        return bh - q.bit_length()
 
     def product(first, size):
         block = gathered[first:first + size, :]
@@ -200,23 +236,59 @@
             sketch_ref[m, :, :] = jnp.dot(wide, rows_here, precision=HIGHEST,
                                           preferred_element_type=F32)
 
-    for s in reversed(range(stages)):
-        size = total >> (s + 1)
-        double(s).start()
-        if s == stages - 1:
-            for r in range(stages):
-                halve(r).wait_send()
-        if s == bh - 1:
+    for t in range(1, nl):
+        low_gather(t).wait_recv()
+    for q in range(nh):
+        if q:
+            stage = came_by(q)
+            pass_on(q - (nh >> (stage + 1)), stage).wait_recv()
+        for s in reversed(range(came_by(q))):
+            pass_on(q, s).start()
+        if q == 0:
             sketch()
-        if s == 0:
-            gram_ref[...] = product(0, size)
-        double(s).wait()
-        if s == 0:
-            gram_ref[...] = (gram_ref[...] + product(size, size)) * (1.0 / total)
+            gram_ref[...] = product(0, span)
+        elif q < nh - 1:
+            gram_ref[...] = gram_ref[...] + product(q * span, span)
+        else:
+            gram_ref[...] = (gram_ref[...] + product(q * span, span)) * (1.0 / total)
+    for t in range(1, nl):
+        low_gather(t).wait_send()
+    for q in range(nh):
+        for s in range(came_by(q)):
+            pass_on(q, s).wait_send()
+
+
+def eliminate(both, hook):
+    nb = both.shape[0]
+    sub = lax.broadcasted_iota(jnp.int32, (8, both.shape[1]), 0)
+    wide = (8, both.shape[1])
+    tiles = [both[8 * g:8 * g + 8, :] for g in range(nb // 8)]
+    for g0 in range(nb // 8):
+        hook()
+        cols = {}
+        for g in range(g0, nb // 8):
+            cols[g] = [jnp.broadcast_to(tiles[g][:, 8 * g0 + j:8 * g0 + j + 1], wide) for j in range(8)]
+        for i in range(8):
+            if i == 7 and g0 == nb // 8 - 1:
+                break
+            lead = cols[g0]
+            flip = 1.0 / lead[i][i:i + 1, :]
+            pivot = tiles[g0][i:i + 1, :]
+            heads = [lead[j][i:i + 1, :] for j in range(8)]
+            for g in range(g0, nb // 8):
+                if g == g0 and i == 7:
+                    continue
+                rate = cols[g][i] * flip
+                if g == g0:
+                    rate = jnp.where(sub > i, rate, 0.0)
+                for j in range(i + 1, 8):
+                    cols[g][j] = cols[g][j] - rate * heads[j]
+                tiles[g] = tiles[g] - rate * pivot
+    return jnp.concatenate(tiles, axis=0)
 
 
 def factor_kernel(gram_ref, sketch_in, current_ref, sketch_ref, r_ref, out_ref,
-                  xbuf, obuf, load_sem, store_sem):
+                  xbuf, parts, obuf, load_sem, store_sem):
     rows, width = current_ref.shape
     pieces = 8
     step = rows // pieces
@@ -237,30 +309,35 @@
 
     n = width
     blocks = n // BLOCK
+    hooks = blocks * (BLOCK // 8)
+    slab = rows // (hooks - BLOCK // 8)
+    state = {"next": 0, "turn": 0}
+
+    def split():
+        state["turn"] += 1
+        if state["turn"] <= BLOCK // 8 or state["next"] >= rows:
+            return
+        first = state["next"]
+        last = min(rows, first + -(-slab // 16) * 16)
+        state["next"] = last
+        x = xbuf[first:last, :]
+        top = x.astype(BF16)
+        parts[first:last, 0:width] = top
+        parts[first:last, width:2 * width] = (x - top.astype(F32)).astype(BF16)
+
     row = lax.broadcasted_iota(jnp.int32, (BLOCK, n), 0)
     col = lax.broadcasted_iota(jnp.int32, (BLOCK, n), 1)
     a = [gram_ref[k * BLOCK:(k + 1) * BLOCK, :] for k in range(blocks)]
     w = [jnp.where(row + k * BLOCK == col, 1.0, 0.0).astype(F32) for k in range(blocks)]
-    sub = lax.broadcasted_iota(jnp.int32, (8, 2 * BLOCK), 0)
     small_row = lax.broadcasted_iota(jnp.int32, (BLOCK, BLOCK), 0)
     small_col = lax.broadcasted_iota(jnp.int32, (BLOCK, BLOCK), 1)
     unit = jnp.where(small_row == small_col, 1.0, 0.0).astype(F32)
     for k in range(blocks):
         at = slice(k * BLOCK, (k + 1) * BLOCK)
-        both = jnp.concatenate([a[k][:, at], unit], axis=1)
-        tiles = [both[8 * g:8 * g + 8, :] for g in range(BLOCK // 8)]
-        for i in range(BLOCK - 1):
-            g0, r0 = i // 8, i % 8
-            pivot = tiles[g0][r0:r0 + 1, :]
-            scaled = pivot / tiles[g0][r0:r0 + 1, i:i + 1]
-            for g in range(g0, BLOCK // 8):
-                if g == g0 and r0 == 7:
-                    continue
-                drop = tiles[g][:, i:i + 1] * scaled
-                if g == g0:
-                    drop = jnp.where(sub > r0, drop, 0.0)
-                tiles[g] = tiles[g] - drop
-        both = jnp.concatenate(tiles, axis=0)
+        if k == 1:
+            for c in range(pieces):
+                load(c).wait()
+        both = eliminate(jnp.concatenate([a[k][:, at], unit], axis=1), split)
         diag = jnp.sum(jnp.where(small_row == small_col, both[:, :BLOCK], 0.0), axis=1, keepdims=True)
         scale = 1.0 / jnp.sqrt(diag)
         inv = both[:, BLOCK:] * scale
@@ -276,16 +353,12 @@
     inverse = jnp.concatenate(w, axis=0).T
     top = inverse.astype(BF16)
     rest = (inverse - top.astype(F32)).astype(BF16)
+    stack = jnp.concatenate([top, top, rest], axis=0)
     for c in range(pieces):
-        load(c).wait()
         at = slice(c * step, (c + 1) * step)
-        x = xbuf[at, :]
-        x_top = x.astype(BF16)
-        x_rest = (x - x_top.astype(F32)).astype(BF16)
-        y = jnp.dot(x_top, rest, preferred_element_type=F32)
-        y = y + jnp.dot(x_rest, top, preferred_element_type=F32)
-        y = y + jnp.dot(x_top, top, preferred_element_type=F32)
-        obuf[at, :] = y
+        x = parts[at, :]
+        x = jnp.concatenate([x, x[:, 0:width]], axis=1)
+        obuf[at, :] = jnp.dot(x, stack, preferred_element_type=F32)
         store(c).start()
     for c in range(pieces):
         store(c).wait()
@@ -297,9 +370,6 @@
     devices = nh * nl
     total = devices * count
     stages = bits_of(devices)
-    own = lax.axis_index("hi") * nl + lax.axis_index("lo")
-    note = jnp.concatenate([own * rows + sample_rows, sample_owner[:, 0]])
-    note = jnp.pad(note.astype(F32), (0, LANES - 2 * count))[None, :]
     vmem = pl.BlockSpec(memory_space=pltpu.VMEM)
     anywhere = pl.BlockSpec(memory_space=pl.ANY)
     dma = pltpu.SemaphoreType.DMA
@@ -309,9 +379,10 @@
         name="mix",
         out_shape=(jax.ShapeDtypeStruct((width, width), F32),
                    jax.ShapeDtypeStruct((MOST, nl, width), F32)),
-        in_specs=[vmem, vmem, anywhere],
+        in_specs=[vmem, vmem, vmem, anywhere],
         out_specs=(vmem, vmem),
         scratch_shapes=[
+            pltpu.VMEM((1, LANES), F32),
             pltpu.VMEM((rows, width), F32),
             pltpu.VMEM((rows, width), BF16),
             pltpu.VMEM((rows, width), BF16),
@@ -319,13 +390,15 @@
             pltpu.VMEM((chunk, rows), BF16),
             pltpu.VMEM((total, width), F32),
             pltpu.VMEM((total, width), F32),
+            pltpu.VMEM((nl, count, width), F32),
             pltpu.VMEM((total, width), F32),
             dma((8,)), dma((devices,)), dma((devices,)),
-            dma((stages,)), dma((stages,)), dma((stages,)), dma((stages,)),
+            dma((stages,)), dma((stages,)), dma((nl,)), dma((nl,)), dma((nl,)), dma((nl,)),
+            dma((stages * nh,)), dma((stages * nh,)),
         ],
         compiler_params=pltpu.CompilerParams(
-            collective_id=0, has_side_effects=True, vmem_limit_bytes=48 * 2 ** 20),
-    )(note, signs.reshape(rows // LANES, LANES), current)
+            collective_id=0, has_side_effects=True, vmem_limit_bytes=VMEM_LIMIT),
+    )(sample_rows.reshape(1, count), sample_owner, signs.reshape(rows // LANES, LANES), current)
     sketch, r_factor, precond = pl.pallas_call(
         factor_kernel,
         name="factor",
@@ -336,10 +409,11 @@
         out_specs=(vmem, vmem, anywhere),
         scratch_shapes=[
             pltpu.VMEM((rows, width), F32),
+            pltpu.VMEM((rows, 2 * width), BF16),
             pltpu.VMEM((rows, width), F32),
             dma((8,)), dma((8,)),
         ],
-        compiler_params=pltpu.CompilerParams(vmem_limit_bytes=48 * 2 ** 20),
+        compiler_params=pltpu.CompilerParams(vmem_limit_bytes=VMEM_LIMIT),
     )(gram, picked, current)
     return (sketch.reshape(1, 1, nl, MOST, width), r_factor, precond)
 

time: 80.7 us -> 54.9 us (0.68)
  Pallas kernels: 75.4 us -> 52.6 us
  local copies, waits for them, and re-layouts: 2.91 us -> 1.33 us
  other arithmetic: 1.39 us -> 0 us
    pallas_call x1, Pallas kernels: 30.5 us -> 15.5 us  [shards(): pl.pallas_call(factor_kernel, name='factor', out_shape=(jax.ShapeDtypeStr...]
    pallas_call x1, Pallas kernels: 44.9 us -> 37.2 us  [shards(): pl.pallas_call(functools.partial(mix_kernel, nh, nl, count), name='mix',...]
    unnamed x6 -> x1, local copies, waits for them, and re-layouts: 2.91 us -> 1.33 us
where the time goes in v2:
time: 54.9 us; the launch traced here: 54.6 us
  Pallas kernels  52.6 us (96%)
  local copies, waits for them, and re-layouts  1.33 us (2%)
  between operations  0.64 us (1%)
    pallas_call x1, Pallas kernels, shards(): pl.pallas_call(functools.partial(mix_kernel, nh, nl, count), name='mix',...  37.2 us
    pallas_call x1, Pallas kernels, shards(): pl.pallas_call(factor_kernel, name='factor', out_shape=(jax.ShapeDtypeStr...  15.5 us
    unnamed x1, local copies, waits for them, and re-layouts  1.33 us

profile of v2, /device:TPU:0, one launch (start us, length us, event | category | flops | bytes accessed | tf_op | source)
XLA Modules:
  0.0 54.6 jit_solution(4589864494498316435)
XLA Ops:
  0.6 1.3 %copy.7.owner_ref = s32[16,1]{1,0:T(8,128)} copy(s32[16,1]{0,1:T(1,128)} %param.7) | data formatting | bytes 128 | tf_op args[3]
  2.0 37.2 %mix.1 = (f32[256,256]{1,0:T(8,128)}, f32[2,8,256]{2,1,0:T(8,128)}) custom-call(s32[1,16]{1,0:T(1,128)} %bitcast.4, s32[16,1]{1,0:T(8,128)} %copy.7.owner_ref, s32[32,128]{1,0:T(8,128)} %bitcast.3, f32[4096,256]{1,0:T(8,128)} %current_ref.3), custom_call_target="tpu_custom_call" | custom-call | tf_op jit(solution)/shard_map/mix/pallas_call | solution.py:377
  39.1 15.5 %factor.1 = (f32[8,2,256]{2,1,0:T(2,128)}, f32[256,256]{1,0:T(8,128)}, f32[4096,256]{1,0:T(8,128)}) custom-call(f32[256,256]{1,0:T(8,128)} %get-tuple-element.8.gram_ref, f32[2,8,256]{2,1,0:T(8,128)} %get-tuple-element.9.sketch_in, f32[4096,256]{1,0:T(8,128)} %current_ref.3), custom_call_target="tpu_custom_call" | custom-call | tf_op jit(solution)/shard_map/factor/pallas_call | solution.py:402

commit v3 on v2

--- a/solution.py
+++ b/solution.py
@@ -39,9 +39,9 @@
     return value & 1
 
 
-def mix_kernel(nh, nl, count, rows_ref, owner_ref, signs_ref, current_ref, gram_ref, sketch_ref,
-               note_ref, xbuf, xhi, xlo, notes, mat, share, landed, shared, gathered,
-               load_sem, nsend, nrecv, rsend, rrecv, lsend, lrecv, asend, arecv, gsend, grecv):
+def mix_kernel(nh, nl, count, rows_hbm, owner_hbm, signs_hbm, current_ref, gram_ref, sketch_ref,
+               rows_ref, owner_ref, signs_ref, note_ref, xbuf, xhi, xlo, notes, mat, share, landed, shared, gathered,
+               small_sem, load_sem, nsend, nrecv, rsend, rrecv, lsend, lrecv, asend, arecv, gsend, grecv):
     hi, lo = lax.axis_index("hi"), lax.axis_index("lo")
     own = hi * nl + lo
     bh, bl = bits_of(nh), bits_of(nl)
@@ -57,15 +57,11 @@
         at = pl.ds(c * step, step)
         return pltpu.make_async_copy(current_ref.at[at, :], xbuf.at[at, :], load_sem.at[c])
 
-    for c in range(loads):
-        load(c).start()
-
-    tags = lax.broadcasted_iota(jnp.int32, (count, LANES), 1)
-    spots = lax.broadcasted_iota(jnp.int32, (count, LANES), 0)
-    named = jnp.broadcast_to(owner_ref[...].astype(F32), (count, LANES))
-    named = jnp.where(tags == spots + count, named, 0.0)
-    note_ref[...] = jnp.sum(named, axis=0, keepdims=True)
-    note_ref[:, 0:count] = (rows_ref[...] + own * rows).astype(F32)
+    small = [pltpu.make_async_copy(source, target, small_sem.at[k])
+             for k, (source, target) in enumerate(
+                 ((rows_hbm, rows_ref), (owner_hbm, owner_ref), (signs_hbm, signs_ref)))]
+    for copy in small:
+        copy.start()
 
     def peer(t):
         return (hi ^ (t >> bl), lo ^ (t & (nl - 1)))
@@ -76,6 +72,13 @@
     barrier = pltpu.get_barrier_semaphore()
     for t in range(1, devices):
         pl.semaphore_signal(barrier, inc=1, device_id=peer(t), device_id_type=MESH)
+    for c in range(loads):
+        load(c).start()
+    for copy in small:
+        copy.wait()
+    note_ref[...] = jnp.zeros_like(note_ref)
+    note_ref[:, 0:count] = (rows_ref[...] + own * rows).astype(F32)
+    note_ref[:, count:2 * count] = owner_ref[...].astype(F32)
     pl.semaphore_wait(barrier, devices - 1)
 
     def note(t):
@@ -342,12 +345,16 @@
         scale = 1.0 / jnp.sqrt(diag)
         inv = both[:, BLOCK:] * scale
         r_rows = jnp.dot(inv, a[k], precision=HIGHEST, preferred_element_type=F32)
+        lower = {}
+        for later in range(k + 1, blocks):
+            lower[later] = lax.dot_general(a[later][:, at], inv, (((1,), (1,)), ((), ())),
+                                           precision=HIGHEST, preferred_element_type=F32)
+            a[later] = a[later] - jnp.dot(lower[later], r_rows, precision=HIGHEST,
+                                          preferred_element_type=F32)
         w_rows = jnp.dot(inv, w[k], precision=HIGHEST, preferred_element_type=F32)
         for later in range(k + 1, blocks):
-            lower = lax.dot_general(a[later][:, at], inv, (((1,), (1,)), ((), ())),
-                                    precision=HIGHEST, preferred_element_type=F32)
-            a[later] = a[later] - jnp.dot(lower, r_rows, precision=HIGHEST, preferred_element_type=F32)
-            w[later] = w[later] - jnp.dot(lower, w_rows, precision=HIGHEST, preferred_element_type=F32)
+            w[later] = w[later] - jnp.dot(lower[later], w_rows, precision=HIGHEST,
+                                          preferred_element_type=F32)
         r_ref[at, :] = jnp.where(row + k * BLOCK <= col, r_rows, 0.0)
         w[k] = w_rows
     inverse = jnp.concatenate(w, axis=0).T
@@ -379,9 +386,12 @@
         name="mix",
         out_shape=(jax.ShapeDtypeStruct((width, width), F32),
                    jax.ShapeDtypeStruct((MOST, nl, width), F32)),
-        in_specs=[vmem, vmem, vmem, anywhere],
+        in_specs=[anywhere, anywhere, anywhere, anywhere],
         out_specs=(vmem, vmem),
         scratch_shapes=[
+            pltpu.VMEM((1, count), jnp.int32),
+            pltpu.VMEM((1, count), jnp.int32),
+            pltpu.VMEM((rows // LANES, LANES), jnp.int32),
             pltpu.VMEM((1, LANES), F32),
             pltpu.VMEM((rows, width), F32),
             pltpu.VMEM((rows, width), BF16),
@@ -392,13 +402,13 @@
             pltpu.VMEM((total, width), F32),
             pltpu.VMEM((nl, count, width), F32),
             pltpu.VMEM((total, width), F32),
-            dma((8,)), dma((devices,)), dma((devices,)),
+            dma((3,)), dma((8,)), dma((devices,)), dma((devices,)),
             dma((stages,)), dma((stages,)), dma((nl,)), dma((nl,)), dma((nl,)), dma((nl,)),
             dma((stages * nh,)), dma((stages * nh,)),
         ],
         compiler_params=pltpu.CompilerParams(
             collective_id=0, has_side_effects=True, vmem_limit_bytes=VMEM_LIMIT),
-    )(sample_rows.reshape(1, count), sample_owner, signs.reshape(rows // LANES, LANES), current)
+    )(sample_rows.reshape(1, count), sample_owner.reshape(1, count), signs.reshape(rows // LANES, LANES), current)
     sketch, r_factor, precond = pl.pallas_call(
         factor_kernel,
         name="factor",

time: 54.9 us -> 52.6 us (0.958)
  local copies, waits for them, and re-layouts: 1.33 us -> 0 us
  Pallas kernels: 52.6 us -> 51.8 us
    unnamed x1 -> x0, local copies, waits for them, and re-layouts: 1.33 us -> none
    pallas_call x1, Pallas kernels: 37.2 us -> 36.4 us  [shards(): pl.pallas_call(functools.partial(mix_kernel, nh, nl, count), name='mix',...]
where the time goes in v3:
time: 52.6 us; the launch traced here: 52.5 us
  Pallas kernels  51.8 us (98%)
  between operations  0.64 us (1%)
    pallas_call x1, Pallas kernels, shards(): pl.pallas_call(functools.partial(mix_kernel, nh, nl, count), name='mix',...  36.4 us
    pallas_call x1, Pallas kernels, shards(): pl.pallas_call(factor_kernel, name='factor', out_shape=(jax.ShapeDtypeStr...  15.4 us

profile of v3, /device:TPU:0, one launch (start us, length us, event | category | flops | bytes accessed | tf_op | source)
XLA Modules:
  0.0 52.5 jit_solution(8039673236494427112)
XLA Ops:
  0.6 36.4 %mix.1 = (f32[256,256]{1,0:T(8,128)}, f32[2,8,256]{2,1,0:T(8,128)}) custom-call(s32[1,16]{1,0:T(1,128)} %bitcast.5, s32[1,16]{1,0:T(1,128)} %bitcast.6, s32[32,128]{1,0:T(8,128)} %bitcast.4, f32[4096,256]{1,0:T(8,128)} %current_ref.3), custom_call_target="tpu_custom_call" | custom-call | tf_op jit(solution)/shard_map/mix/pallas_call | solution.py:384
  37.1 15.4 %factor.1 = (f32[8,2,256]{2,1,0:T(2,128)}, f32[256,256]{1,0:T(8,128)}, f32[4096,256]{1,0:T(8,128)}) custom-call(f32[256,256]{1,0:T(8,128)} %get-tuple-element.8.gram_ref, f32[2,8,256]{2,1,0:T(8,128)} %get-tuple-element.9.sketch_in, f32[4096,256]{1,0:T(8,128)} %current_ref.3), custom_call_target="tpu_custom_call" | custom-call | tf_op jit(solution)/shard_map/factor/pallas_call | solution.py:412
